TPU v7x, 256 devices: a whole 4x4x8 slice. The times are simulated.
256 devices in a mesh: leaf: 4 (over x), owner: 64 (over z, y, core).
Axes of the slice: x: 4, y: 4, z: 8, core: 2. Of those that a mesh axis runs over, the one named last changes fastest.
Arguments:
- multipoles: float32 [3, 343, 98304], P(None, None, ('leaf', 'owner')), may hold values from -6 to 6
- operators: bfloat16 [4, 1029, 1029], replicated, may hold values from -0.1875 to 0.1875
- lists: int32 [98304, 4], P(('leaf', 'owner')), may hold values from -1 to 671, as said below
- send_slots: int32 [256, 64, 4], P(('leaf', 'owner')), may hold values from -1 to 31, as said below
Outputs:
- locals_out: float32 [3, 343, 98304], P(None, None, ('leaf', 'owner'))
Inputs may be any that keep to these rules, and one draw needn't show every extreme that they name: `lists`: A code of the first kind appears only for boxes of groups other than the first, of the third kind only for groups other than the last; a code naming (p, c) appears only where send_slots of owner p for this owner holds a slot at c, and never with p equal to the box's own owner. `send_slots`: entries are distinct boundary slots followed by -1 padding; the entries for an owner itself are all -1; every draw fills some pair's 4 entries.
All inputs are finite; a program needn't handle non-finite values.
Results may differ from a plain program's by a relative error of at most 0.0029.
Values may be sent and summed in bfloat16 or wider, within the bound.
No kernel may reach another device: no remote copies, remote signals or barrier semaphores. Data moves between devices by JAX's collectives and lax.ppermute only.
A program may use at most 128 MiB of HBM per device.

v0:
```python
import jax
import jax.numpy as jnp
from jax import lax
from jax.sharding import PartitionSpec as P

DIRS = 4
FACE = 16
BOUND = 32


def with_halo(block, sides, width):
    for axis, dim in sides:
        count = lax.axis_size(axis)
        forward = [(i, i + 1) for i in range(count - 1)]
        backward = [(target, source) for source, target in forward]
        low = lax.ppermute(
            lax.slice_in_dim(block, block.shape[dim] - width, None, axis=dim), axis, forward
        )
        high = lax.ppermute(lax.slice_in_dim(block, 0, width, axis=dim), axis, backward)
        block = jnp.concatenate([low, block, high], axis=dim)
    return block


def select_columns(source, wanted):
    positions = lax.broadcasted_iota(jnp.int32, (source.shape[1], wanted.shape[0]), 0)
    selector = (positions == wanted[None, :]).astype(jnp.bfloat16)
    return jnp.dot(source, selector, preferred_element_type=jnp.float32)


def local(multipoles, operators, lists, send_slots):
    comps, nodes, nboxes = multipoles.shape
    width = comps * nodes
    packed = multipoles.reshape(width, nboxes).astype(jnp.bfloat16)
    extended = with_halo(packed, (("leaf", 1),), FACE)
    owners = lax.axis_size("owner")
    boundary = packed[:, :BOUND]
    gathered, all_slots = (
        lax.all_gather(boundary, "owner", axis=1, tiled=True),
        lax.all_gather(send_slots, "owner", axis=0, tiled=True),
    )
    myself = lax.axis_index("owner")
    my_slots = lax.dynamic_index_in_dim(all_slots, myself, 1, keepdims=False)
    offsets = jnp.arange(owners, dtype=jnp.int32)[:, None] * BOUND
    picks = jnp.where(my_slots >= 0, offsets + my_slots, -1).reshape(-1)
    ghost_table = select_columns(gathered, picks).astype(jnp.bfloat16)
    extent = extended.shape[1]
    total = jnp.zeros((width, nboxes), jnp.float32)
    for direction in range(DIRS):
        codes = lists[:, direction]
        near_part = select_columns(extended, codes)
        ghost_part = select_columns(ghost_table, codes - extent)
        columns = (near_part + ghost_part).astype(jnp.bfloat16)
        total = total + jnp.dot(operators[direction], columns, preferred_element_type=jnp.float32)
    return total.reshape(comps, nodes, nboxes)


def solution(mesh):
    return jax.shard_map(
        local,
        mesh=mesh,
        in_specs=(
            P(None, None, ("leaf", "owner")),
            P(),
            P(("leaf", "owner"), None),
            P(("leaf", "owner"), None, None),
        ),
        out_specs=P(None, None, ("leaf", "owner")),
        check_vma=False,
    )
```

profile of v0, /device:TPU:1, one launch (start us, length us, event | category | flops | bytes accessed | tf_op | source)
XLA Modules:
  0.0 141.9 jit_solution(5781420917484974898)
XLA Ops:
  6.5 0.0 all-gather.2.cloned.1.call-start
  6.5 1.5 %convert_element_type.31 = bf16[3,343,384]{2,1,0:T(8,128)(2,1)S(1)} convert(f32[3,343,384]{2,1,0:T(8,128)} %param.4) | non-fusion elementwise | flops 395136 | bytes 2370816 | tf_op jit(solution)/shard_map/convert_element_type | solution.py:33
  8.0 0.0 copy-start.1
  8.1 0.2 convert_element_type.32
  8.3 0.0 copy-start
  8.3 0.8 copy.14
  9.1 0.0 all-gather.2.cloned.1.call-update
  9.1 0.1 fusion.24
  9.3 3.9 %collective-permute-start = (bf16[1029,16]{1,0:T(8,128)(2,1)S(1)}, bf16[1029,16]{1,0:T(8,128)(2,1)S(1)}, u32[]{:S(2)}, u32[]{:S(2)}) collective-permute-start(bf16[1029,16]{1,0:T(8,128)(2,1)S(1)} %get-tuple-element.13), channel_id=1, source_target_pairs={{0,64},{64,128},{128,192},{1,65},{65,129},{129,193},{2,66},{66,130... | collective-permute-start | bytes 98792 | tf_op jit(solution)/shard_map/ppermute | solution.py:16
  13.2 1.3 collective-permute-start.1
  14.5 0.0 copy-done.1
  14.5 54.0 %all_gather.6 = s32[64,64,4]{1,2,0:T(4,128)S(1)} all-gather(s32[1,64,4]{1,2,0:T(4,128)S(1)} %copy-done.1), channel_id=1, replica_groups=mesh['leaf'=4,'owner'=64] {'owner'}, dimensions={0}, use_global_device_ids=true | all-gather | bytes 66560 | tf_op jit(solution)/shard_map/all_gather | solution.py:39
  68.5 1.2 dynamic-slice_reduce_fusion
  69.8 0.1 squeeze.20
  69.9 0.1 add.65
  70.0 0.1 add.66
  70.1 0.0 copy-done
  70.2 27.0 %fusion.23 = (bf16[1,1029,1029]{2,0,1:T(2,128)(2,1)}, bf16[1,1029,1029]{2,0,1:T(2,128)(2,1)}, bf16[1,1029,1029]{2,0,1:T(2,128)(2,1)}, bf16[1,1029,1029]{2,0,1:T(2,128)(2,1)}) fusion(bf16[4,1029,1029]{2,0,1:T(4,128)(2,1)} %param.5), kind=kLoop, calls=%fused_computation.52 | loop fusion | bytes 16941456 | tf_op jit(solution)/shard_map/slice | solution.py:53
  97.1 0.0 all-gather.2.cloned.1.call-done
  97.1 4.2 %convolution_convert_fusion = bf16[256,1029]{0,1:T(8,128)(2,1)S(1)} fusion(bf16[1029,2048]{0,1:T(8,128)(2,1)} %all-gather.2.cloned.1.call-done, s32[256]{0:T(256)S(1)} %compare_select_fusion), kind=kOutput, calls=%fused_computation.12 | convolution fusion | flops 1079772416 | bytes 4742656 | tf_op jit(solution)/shard_map/dot_general | solution.py:27
  101.4 1.6 %fusion.7 = f32[1029,384]{1,0:T(8,128)} fusion(bf16[256,1029]{0,1:T(8,128)(2,1)S(1)} %convolution_convert_fusion, s32[384]{0:T(512)S(1)} %get-tuple-element.18), kind=kOutput, calls=%fused_computation.29 | convolution fusion | flops 202407936 | bytes 2108928 | tf_op jit(solution)/shard_map/dot_general | solution.py:27
  103.0 1.6 %fusion.8 = f32[1029,384]{1,0:T(8,128)} fusion(bf16[256,1029]{0,1:T(8,128)(2,1)S(1)} %convolution_convert_fusion, s32[384]{0:T(512)S(1)} %get-tuple-element.17), kind=kOutput, calls=%fused_computation.30 | convolution fusion | flops 202407936 | bytes 2108928 | tf_op jit(solution)/shard_map/dot_general | solution.py:27
  104.6 1.6 %fusion.9 = f32[1029,384]{1,0:T(8,128)} fusion(bf16[256,1029]{0,1:T(8,128)(2,1)S(1)} %convolution_convert_fusion, s32[384]{0:T(512)S(1)} %get-tuple-element.16), kind=kOutput, calls=%fused_computation.31 | convolution fusion | flops 202407936 | bytes 2108928 | tf_op jit(solution)/shard_map/dot_general | solution.py:27
  106.2 0.5 fusion.10
  106.7 0.0 collective-permute-done
  106.7 0.0 collective-permute-done.1
  106.7 6.2 %fusion.5 = f32[384,1029]{0,1:T(8,128)} fusion(bf16[1,1029,1029]{2,0,1:T(2,128)(2,1)} %get-tuple-element.12, f32[1029,384]{1,0:T(8,128)} %fusion.7, s32[384]{0:T(512)S(1)} %get-tuple-element.7, bf16[1029,16]{1,0:T(8,128)(2,1)S(1)} %collective-permute-done.1, bf16[1029,384]{1,0:T(8,128)(2,1)S(1)} %convert_element_type.32, ...), kind=kOutput, calls=%fused_computation.17 | convolution fusion | flops 1145461504 | bytes 6136434 | tf_op jit(solution)/shard_map/dot_general | solution.py:53
  112.9 6.6 %convolution_add_fusion.6 = f32[384,1029]{0,1:T(8,128)} fusion(f32[384,1029]{0,1:T(8,128)} %fusion.5, bf16[1,1029,1029]{2,0,1:T(2,128)(2,1)} %get-tuple-element.11, f32[1029,384]{1,0:T(8,128)} %fusion.8, s32[384]{0:T(512)S(1)} %get-tuple-element.6, bf16[1029,16]{1,0:T(8,128)(2,1)S(1)} %collective-permute-done.1, ...), kind=kOutput, calls=%fused_computation.6 | convolution fusion | flops 1145856640 | bytes 7716978 | tf_op jit(solution)/shard_map/dot_general | solution.py:53
  119.5 6.6 %convolution_add_fusion.5 = f32[384,1029]{0,1:T(8,128)} fusion(f32[384,1029]{0,1:T(8,128)} %convolution_add_fusion.6, bf16[1,1029,1029]{2,0,1:T(2,128)(2,1)} %get-tuple-element.10, f32[1029,384]{1,0:T(8,128)} %fusion.9, s32[384]{0:T(512)S(1)} %get-tuple-element.8, bf16[1029,16]{1,0:T(8,128)(2,1)S(1)} %collective-permute-done.1, ...), kind=kOutput, calls=%fused_computation.5 | convolution fusion | flops 1145856640 | bytes 7716978 | tf_op jit(solution)/shard_map/dot_general | solution.py:53
  126.2 6.2 %fusion = f32[1029,384]{1,0:T(8,128)} fusion(f32[384,1029]{0,1:T(8,128)} %convolution_add_fusion.5, bf16[1,1029,1029]{2,0,1:T(2,128)(2,1)} %get-tuple-element.9, f32[1029,384]{1,0:T(8,128)S(1)} %fusion.10, s32[384]{0:T(512)S(1)} %get-tuple-element.5, bf16[1029,16]{1,0:T(8,128)(2,1)S(1)} %collective-permute-done.1, ...), kind=kOutput, calls=%fused_computation.7 | convolution fusion | flops 1145856640 | bytes 7716978 | tf_op jit(solution)/shard_map/dot_general | solution.py:53
  132.4 2.7 %reshape.50 = f32[3,343,384]{2,1,0:T(8,128)} reshape(f32[1029,384]{1,0:T(8,128)} %fusion) | data formatting | bytes 3161088 | tf_op jit(solution)/shard_map/reshape | solution.py:54
  (6 shorter events, 0.1 us)
Async XLA Ops:
  6.5 90.6 %all-gather.2.cloned.1.call-start = ((), (), s32[]{:S(2)}) async-start(), calls=%async_computation | async-start | bytes 4792320 | tf_op jit(solution)/shard_map/all_gather | solution.py:38
  8.0 6.5 %copy-start.1 = (s32[1,64,4]{1,2,0:T(4,128)S(1)}, s32[1,64,4]{1,2,0:T(4,128)}, u32[]{:S(2)}) copy-start(s32[1,64,4]{1,2,0:T(4,128)} %param.7) | copy-start | bytes 3076
  8.3 61.8 %copy-start = (s32[384,4]{0,1:T(4,128)S(1)}, s32[384,4]{0,1:T(4,128)}, u32[]{:S(2)}) copy-start(s32[384,4]{0,1:T(4,128)} %param.6) | copy-start | bytes 18436
  9.3 97.4 %collective-permute-start = (bf16[1029,16]{1,0:T(8,128)(2,1)S(1)}, bf16[1029,16]{1,0:T(8,128)(2,1)S(1)}, u32[]{:S(2)}, u32[]{:S(2)}) collective-permute-start(bf16[1029,16]{1,0:T(8,128)(2,1)S(1)} %get-tuple-element.13), channel_id=1, source_target_pairs={{0,64},{64,128},{128,192},{1,65},{65,129},{129,193},{2,66},{66,130... | collective-permute-start | bytes 98792 | tf_op jit(solution)/shard_map/ppermute | solution.py:16
  13.2 93.5 %collective-permute-start.1 = (bf16[1029,16]{1,0:T(8,128)(2,1)S(1)}, bf16[1029,16]{1,0:T(8,128)(2,1)S(1)}, u32[]{:S(2)}, u32[]{:S(2)}) collective-permute-start(bf16[1029,16]{1,0:T(8,128)(2,1)S(1)} %get-tuple-element.14), channel_id=1, source_target_pairs={{64,0},{128,64},{192,128},{65,1},{129,65},{193,129},{66,2},{130,66... | collective-permute-start | bytes 98792 | tf_op jit(solution)/shard_map/ppermute | solution.py:19
Sparse Core Ops, SparseCore 0:
  10.1 83.2 all-gather.1
where the time goes:
time: 142 us
  blocking collectives  54 us (38%)
  matrix products  35.2 us (25%)
  local copies, waits for them, and re-layouts  32.4 us (23%)
  between operations  13.5 us (10%)
  starting transfers between devices  5.24 us (4%)
  other arithmetic  1.52 us (1%)
    all_gather x1, blocking collectives, local(): lax.all_gather(send_slots, 'owner', axis=0, tiled=True)  54 us
    slice x1, local copies, waits for them, and re-layouts, local(): operators[direction]  27 us
    dot_general x4, matrix products, local(): jnp.dot(operators[direction], columns, preferred_element_type=jnp.float32)  25.7 us
    dot_general x5, matrix products, select_columns(): return jnp.dot(source, selector, preferred_element_type=jnp.float32)  9.55 us
    ppermute x1, starting transfers between devices, with_halo(): lax.ppermute(lax.slice_in_dim(block, block.shape[dim] - width, None, axis...  3.95 us
  transfers between devices with their start and end apart: 3, of which 0 were waited for; matrix products, arithmetic and copies ran while one was open for 27% of the time, Pallas kernels for 0%

commit v1 on v0

v1 whole, which is shorter than its diff:
```python
import jax
import jax.numpy as jnp
from jax import lax
from jax.experimental import pallas as pl
from jax.experimental.pallas import tpu as pltpu
from jax.sharding import PartitionSpec as P

FACE = 16
LANES = 128
NT = (((1,), (1,)), ((), ()))


def table_kernel(first_ref, last_ref, slots_ref, table_ref, low_ref, high_ref, stage):
    comps, nodes, lanes = first_ref.shape
    cap, owners = slots_ref.shape
    rows = owners * cap
    for comp in range(comps):
        stage[pl.ds(comp * nodes, nodes), :lanes] = first_ref[comp]
        stage[pl.ds(comp * nodes, nodes), lanes:] = last_ref[comp]
    boundary = stage[...].astype(jnp.bfloat16)
    row = lax.broadcasted_iota(jnp.int32, (rows, owners), 0)
    owner = lax.broadcasted_iota(jnp.int32, (rows, owners), 1)
    spread = (row // cap == owner).astype(jnp.bfloat16)
    slots = slots_ref[...].astype(jnp.float32).astype(jnp.bfloat16)
    every = lax.dot_general(spread, slots, NT, preferred_element_type=jnp.float32)
    place = lax.broadcasted_iota(jnp.int32, (rows, cap), 1)
    turn = lax.broadcasted_iota(jnp.int32, (rows, cap), 0) % cap
    wanted = jnp.sum(jnp.where(place == turn, every, 0.0), axis=1, keepdims=True)
    slot = lax.broadcasted_iota(jnp.int32, (rows, 2 * lanes), 1).astype(jnp.float32)
    pick = (slot == wanted).astype(jnp.bfloat16)
    column = lax.broadcasted_iota(jnp.int32, (2 * FACE, 2 * lanes), 1)
    face = lax.broadcasted_iota(jnp.int32, (2 * FACE, 2 * lanes), 0)
    face = jnp.where(face < FACE, face + (2 * lanes - FACE), face - FACE)
    pick = jnp.concatenate([pick, (column == face).astype(jnp.bfloat16)], axis=0)
    table = lax.dot_general(pick, boundary, NT, preferred_element_type=jnp.float32).astype(jnp.bfloat16)
    table_ref[...] = table[:rows].reshape(table_ref.shape)
    low_ref[...] = table[rows:rows + FACE]
    high_ref[...] = table[rows + FACE:]


def make_table(multipoles, slots):
    comps, nodes, nboxes = multipoles.shape
    cap, owners = slots.shape
    width = comps * nodes
    last = nboxes // LANES - 1
    return pl.pallas_call(
        table_kernel,
        out_shape=(
            jax.ShapeDtypeStruct((owners, cap, width), jnp.bfloat16),
            jax.ShapeDtypeStruct((FACE, width), jnp.bfloat16),
            jax.ShapeDtypeStruct((FACE, width), jnp.bfloat16),
        ),
        grid=(1,),
        in_specs=[
            pl.BlockSpec((comps, nodes, LANES), lambda i: (0, 0, 0)),
            pl.BlockSpec((comps, nodes, LANES), lambda i: (0, 0, last)),
            pl.BlockSpec((cap, owners), lambda i: (0, 0)),
        ],
        out_specs=(
            pl.BlockSpec((owners, cap, width), lambda i: (0, 0, 0)),
            pl.BlockSpec((FACE, width), lambda i: (0, 0)),
            pl.BlockSpec((FACE, width), lambda i: (0, 0)),
        ),
        scratch_shapes=[pltpu.VMEM((width, 2 * LANES), jnp.float32)],
        name="table",
    )(multipoles, multipoles, slots)


def spread_out(y, spread, comp):
    for t in range(spread.shape[1]):
        spread[comp, t] = y[:, t * LANES:(t + 1) * LANES]


def gather_in(spread, picks, comp, dirs, nodes):
    pieces = [
        spread[comp, t, pl.ds(d, nodes, stride=dirs), :]
        for d in range(dirs)
        for t in range(spread.shape[1])
    ]
    moved = jnp.concatenate(pieces, axis=1).astype(jnp.bfloat16)
    return jnp.dot(moved, picks[...], preferred_element_type=jnp.float32)


def near_kernel(m_hbm, low_ref, high_ref, codes_ref, a_hbm, near_hbm, stage, source, picks, spread, held, total, sems, m_sems, out_sems):
    comps, nodes, nboxes = m_hbm.shape
    dirs, width = a_hbm.shape[1:]
    wide = picks.shape[0] // dirs

    def fetch(comp):
        return pltpu.make_async_copy(a_hbm.at[pl.ds(comp * nodes, nodes)], held.at[comp], sems.at[comp])

    def fetch_m(comp):
        return pltpu.make_async_copy(m_hbm.at[comp], total.at[comp], m_sems.at[comp])

    def store(comp):
        return pltpu.make_async_copy(total.at[comp], near_hbm.at[comp], out_sems.at[comp])

    for comp in range(comps):
        fetch_m(comp).start()
    for comp in range(comps):
        fetch(comp).start()
    blank = jnp.zeros((wide - nboxes - 2 * FACE, width), jnp.bfloat16)
    source[:, nboxes:] = jnp.concatenate([low_ref[...], high_ref[...], blank], axis=0).T
    place = lax.broadcasted_iota(jnp.int32, (wide, nboxes), 0)
    for d in range(dirs):
        code = codes_ref[pl.ds(d, 1), :]
        low = jnp.where(code < FACE, code + nboxes, code - FACE)
        wanted = jnp.where(code < nboxes + FACE, low, code)
        wanted = jnp.where((code < 0) | (code >= nboxes + 2 * FACE), -1, wanted)
        picks[pl.ds(d * wide, wide), :] = (place == wanted).astype(jnp.bfloat16)
    for comp in range(comps):
        fetch_m(comp).wait()
        stage[pl.ds(comp * nodes, nodes), :] = total[comp]
    source[:, :nboxes] = stage[...].astype(jnp.bfloat16)

    @pl.loop(0, comps)
    def _(comp):
        fetch(comp).wait()
        a = held[comp].reshape(nodes * dirs, width)
        spread_out(jnp.dot(a, source[...], preferred_element_type=jnp.float32), spread, comp)

    @pl.loop(0, comps)
    def _(comp):
        total[comp] = gather_in(spread, picks, comp, dirs, nodes)
        store(comp).start()

    @pl.loop(0, comps)
    def _(comp):
        store(comp).wait()


def far_kernel(near_hbm, g_ref, codes_ref, a_hbm, out_hbm, source, picks, spread, held, total, sems, near_sems, out_sems):
    comps, nodes, nboxes = near_hbm.shape
    dirs = a_hbm.shape[1]
    width = a_hbm.shape[2]
    wide = picks.shape[0] // dirs

    def fetch(comp):
        return pltpu.make_async_copy(a_hbm.at[pl.ds(comp * nodes, nodes)], held.at[comp], sems.at[comp])

    def fetch_near(comp):
        return pltpu.make_async_copy(near_hbm.at[comp], total.at[comp], near_sems.at[comp])

    def store(comp):
        return pltpu.make_async_copy(total.at[comp], out_hbm.at[comp], out_sems.at[comp])

    for comp in range(comps):
        fetch(comp).start()
    for comp in range(comps):
        fetch_near(comp).start()
    source[...] = g_ref[...].reshape(source.shape[1], source.shape[0]).T
    place = lax.broadcasted_iota(jnp.int32, (wide, nboxes), 0) + (nboxes + 2 * FACE)
    for d in range(dirs):
        picks[pl.ds(d * wide, wide), :] = (place == codes_ref[pl.ds(d, 1), :]).astype(jnp.bfloat16)

    @pl.loop(0, comps + 1)
    def _(comp):
        @pl.when(comp < comps)
        def _():
            fetch(comp).wait()
            a = held[comp].reshape(nodes * dirs, width)
            spread_out(jnp.dot(a, source[...], preferred_element_type=jnp.float32), spread, comp)

        @pl.when(comp > 0)
        def _():
            last = comp - 1
            fetch_near(last).wait()
            total[last] = total[last] + gather_in(spread, picks, last, dirs, nodes)
            store(last).start()

    @pl.loop(0, comps)
    def _(comp):
        store(comp).wait()


HBM = pl.BlockSpec(memory_space=pltpu.MemorySpace.HBM)
VMEM = pl.BlockSpec(memory_space=pltpu.MemorySpace.VMEM)


def near_sum(multipoles, low, high, codes, rows):
    comps, nodes, nboxes = multipoles.shape
    width, dirs, _ = rows.shape
    wide = nboxes + LANES
    return pl.pallas_call(
        near_kernel,
        out_shape=jax.ShapeDtypeStruct((comps, nodes, nboxes), jnp.float32),
        in_specs=[HBM, VMEM, VMEM, VMEM, HBM],
        out_specs=HBM,
        scratch_shapes=[
            pltpu.VMEM((width, nboxes), jnp.float32),
            pltpu.VMEM((width, wide), jnp.bfloat16),
            pltpu.VMEM((dirs * wide, nboxes), jnp.bfloat16),
            pltpu.VMEM((comps, wide // LANES, nodes * dirs, LANES), jnp.float32),
            pltpu.VMEM((comps, nodes, dirs, width), jnp.bfloat16),
            pltpu.VMEM((comps, nodes, nboxes), jnp.float32),
            pltpu.SemaphoreType.DMA((comps,)),
            pltpu.SemaphoreType.DMA((comps,)),
            pltpu.SemaphoreType.DMA((comps,)),
        ],
        compiler_params=pltpu.CompilerParams(vmem_limit_bytes=52 << 20),
        name="near",
    )(multipoles, low, high, codes, rows)


def far_sum(near, ghost, codes, rows):
    comps, nodes, nboxes = near.shape
    width, dirs, _ = rows.shape
    owners, cap, _ = ghost.shape
    wide = owners * cap
    return pl.pallas_call(
        far_kernel,
        out_shape=jax.ShapeDtypeStruct((comps, nodes, nboxes), jnp.float32),
        in_specs=[HBM, VMEM, VMEM, HBM],
        out_specs=HBM,
        scratch_shapes=[
            pltpu.VMEM((width, wide), jnp.bfloat16),
            pltpu.VMEM((dirs * wide, nboxes), jnp.bfloat16),
            pltpu.VMEM((comps, wide // LANES, nodes * dirs, LANES), jnp.float32),
            pltpu.VMEM((comps, nodes, dirs, width), jnp.bfloat16),
            pltpu.VMEM((comps, nodes, nboxes), jnp.float32),
            pltpu.SemaphoreType.DMA((comps,)),
            pltpu.SemaphoreType.DMA((comps,)),
            pltpu.SemaphoreType.DMA((comps,)),
        ],
        compiler_params=pltpu.CompilerParams(vmem_limit_bytes=52 << 20),
        name="far",
    )(near, ghost, codes, rows)


def local(multipoles, operators, lists, send_slots):
    slots = jnp.transpose(send_slots[0])
    table, low, high = make_table(multipoles, slots)
    ghost = lax.all_to_all(table, "owner", 0, 0, tiled=True)
    count = lax.axis_size("leaf")
    forward = [(i, i + 1) for i in range(count - 1)]
    backward = [(target, source) for source, target in forward]
    low = lax.ppermute(low, "leaf", forward)
    high = lax.ppermute(high, "leaf", backward)
    codes = jnp.transpose(lists)
    rows = jnp.transpose(operators, (1, 0, 2))
    near = near_sum(multipoles, low, high, codes, rows)
    return far_sum(near, ghost, codes, rows)


def solution(mesh):
    return jax.shard_map(
        local,
        mesh=mesh,
        in_specs=(
            P(None, None, ("leaf", "owner")),
            P(),
            P(("leaf", "owner"), None),
            P(("leaf", "owner"), None, None),
        ),
        out_specs=P(None, None, ("leaf", "owner")),
        check_vma=False,
    )
```

time: 142 us -> 45.6 us (0.32)
  blocking collectives: 54 us -> 0 us
  matrix products: 35.2 us -> 0 us
  local copies, waits for them, and re-layouts: 32.4 us -> 1.15 us
  Pallas kernels: 0 us -> 22.6 us
  between operations: 13.5 us -> 0.04 us
  starting transfers between devices: 5.24 us -> 17.6 us
  waiting for transfers between devices: 0.03 us -> 3.91 us
  other arithmetic: 1.52 us -> 0 us
    all_gather x1 -> x0, blocking collectives: 54 us -> none  [local(): lax.all_gather(send_slots, 'owner', axis=0, tiled=True)]
    dot_general x9 -> x0, matrix products: 35.2 us -> none  [the longest x4 25.7 us: local(): jnp.dot(operators[direction], columns, preferred_element_type=jnp.float32)]
    slice x5 -> x0, local copies, waits for them, and re-layouts: 27.9 us -> none  [the longest x1 27 us: local(): operators[direction]]
    pallas_call x0 -> x3, Pallas kernels: none -> 22.6 us  [the longest x1 12.3 us: near_sum(): pl.pallas_call(near_kernel, out_shape=jax.ShapeDtypeStruct((comps, nodes,...]
    all_to_all x0 -> x1, starting transfers between devices: none -> 13.1 us  [local(): ghost = lax.all_to_all(table, 'owner', 0, 0, tiled=True)]
    ppermute x2, waiting for transfers between devices: 0.01 us -> 3.91 us  [the longest x1 3.85 us: local(): high = lax.ppermute(high, 'leaf', backward)]
    reshape x1 -> x0, local copies, waits for them, and re-layouts: 2.73 us -> none  [local(): return total.reshape(comps, nodes, nboxes)]
    convert_element_type x1 -> x0, other arithmetic: 1.5 us -> none  [local(): packed = multipoles.reshape(width, nboxes).astype(jnp.bfloat16)]
  transfers between devices with their start and end apart: 3 -> 3, of which waited for: 0 -> 2; matrix products, arithmetic and copies ran while one was open for 27% -> 0% of each run, Pallas kernels for 0% -> 27%
where the time goes in v1:
time: 45.6 us; the launch traced here: 45.3 us
  Pallas kernels  22.6 us (50%)
  starting transfers between devices  17.6 us (39%)
  waiting for transfers between devices  3.91 us (9%)
  local copies, waits for them, and re-layouts  1.15 us (3%)
    all_to_all x1, starting transfers between devices, local(): ghost = lax.all_to_all(table, 'owner', 0, 0, tiled=True)  13.1 us
    pallas_call x1, Pallas kernels, near_sum(): pl.pallas_call(near_kernel, out_shape=jax.ShapeDtypeStruct((comps, nodes,...  12.3 us
    pallas_call x1, Pallas kernels, far_sum(): pl.pallas_call(far_kernel, out_shape=jax.ShapeDtypeStruct((comps, nodes,...  7.76 us
    ppermute x1, waiting for transfers between devices, local(): high = lax.ppermute(high, 'leaf', backward)  3.85 us
    ppermute x1, starting transfers between devices, local(): low = lax.ppermute(low, 'leaf', forward)  3.12 us
    pallas_call x1, Pallas kernels, make_table(): pl.pallas_call(table_kernel, out_shape=(jax.ShapeDtypeStruct((owners, cap...  2.56 us
    ppermute x1, starting transfers between devices, local(): high = lax.ppermute(high, 'leaf', backward)  1.29 us
    unnamed x4, local copies, waits for them, and re-layouts  1.15 us
  transfers between devices with their start and end apart: 3, of which 2 were waited for; matrix products, arithmetic and copies ran while one was open for 0% of the time, Pallas kernels for 27%

profile of v1, /device:TPU:1, one launch (start us, length us, event | category | flops | bytes accessed | tf_op | source)
XLA Modules:
  0.0 45.3 jit_solution(10443488448557917161)
XLA Ops:
  0.0 0.0 copy-start.1
  0.0 2.6 %table.1 = (bf16[64,4,1029]{2,1,0:T(4,128)(2,1)}, bf16[16,1029]{1,0:T(8,128)(2,1)}, bf16[16,1029]{1,0:T(8,128)(2,1)}) custom-call(f32[3,343,384]{2,1,0:T(8,128)} %m_hbm.1, f32[3,343,384]{2,1,0:T(8,128)} %m_hbm.1, s32[4,64]{1,0:T(4,128)} %bitcast.9), custom_call_target="tpu_custom_call" | custom-call | tf_op jit(solution)/shard_map/table/pallas_call | solution.py:46
  2.6 13.1 %all-to-all-start = ((bf16[64,4,1029]{2,1,0:T(4,128)(2,1)}), bf16[64,4,1029]{2,1,0:T(4,128)(2,1)S(1)}, u32[]{:S(2)}, u32[]{:S(2)}) async-start(bf16[64,4,1029]{2,1,0:T(4,128)(2,1)} %get-tuple-element.10), calls=%async_computation | async-start | bytes 1179648 | tf_op jit(solution)/shard_map/all_to_all | solution.py:233
  15.7 3.1 %collective-permute-start = (bf16[16,1029]{1,0:T(8,128)(2,1)}, bf16[16,1029]{1,0:T(8,128)(2,1)S(1)}, u32[]{:S(2)}, u32[]{:S(2)}) collective-permute-start(bf16[16,1029]{1,0:T(8,128)(2,1)} %get-tuple-element.8), channel_id=1, source_target_pairs={{0,64},{64,128},{128,192},{1,65},{65,129},{129,193},{2,66},{66,130... | collective-permute-start | bytes 98792 | tf_op jit(solution)/shard_map/ppermute | solution.py:237
  18.8 1.3 %collective-permute-start.1 = (bf16[16,1029]{1,0:T(8,128)(2,1)}, bf16[16,1029]{1,0:T(8,128)(2,1)S(1)}, u32[]{:S(2)}, u32[]{:S(2)}) collective-permute-start(bf16[16,1029]{1,0:T(8,128)(2,1)} %get-tuple-element.9), channel_id=1, source_target_pairs={{64,0},{128,64},{192,128},{65,1},{129,65},{193,129},{66,2},{130,66... | collective-permute-start | bytes 98792 | tf_op jit(solution)/shard_map/ppermute | solution.py:238
  20.1 0.1 collective-permute-done.low_ref
  20.2 3.8 %collective-permute-done.1.high_ref = bf16[16,1029]{1,0:T(8,128)(2,1)S(1)} collective-permute-done((bf16[16,1029]{1,0:T(8,128)(2,1)}, bf16[16,1029]{1,0:T(8,128)(2,1)S(1)}, u32[]{:S(2)}, u32[]{:S(2)}) %collective-permute-start.1) | collective-permute-done | bytes 32960 | tf_op jit(solution)/shard_map/ppermute | solution.py:238
  24.1 0.0 copy-done.1
  24.1 12.3 %near.1.near_hbm = f32[3,343,384]{2,1,0:T(8,128)S(1)} custom-call(f32[3,343,384]{2,1,0:T(8,128)} %m_hbm.1, bf16[16,1029]{1,0:T(8,128)(2,1)S(1)} %collective-permute-done.low_ref, bf16[16,1029]{1,0:T(8,128)(2,1)S(1)} %collective-permute-done.1.high_ref, s32[4,384]{1,0:T(4,128)S(1)} %bitcast.5, bf16[1029,4,1029]{2,1,0:T(4,128)(2,1)} %bitcast.7), custom_call_target="tpu_custom_call" | custom-call | tf_op jit(solution)/shard_map/near/pallas_call | solution.py:184
  36.4 0.0 copy-start
  36.4 1.1 %copy-done = f32[3,343,384]{2,1,0:T(8,128)} copy-done((f32[3,343,384]{2,1,0:T(8,128)}, f32[3,343,384]{2,1,0:T(8,128)S(1)}, u32[]{:S(2)}) %copy-start) | copy-done | bytes 1580568
  37.5 0.0 all-to-all-done.g_ref
  37.5 7.8 %far.1 = f32[3,343,384]{2,1,0:T(8,128)} custom-call(f32[3,343,384]{2,1,0:T(8,128)} %copy-done, bf16[64,4,1029]{2,1,0:T(4,128)(2,1)S(1)} %all-to-all-done.g_ref, s32[4,384]{1,0:T(4,128)S(1)} %bitcast.6, bf16[1029,4,1029]{2,1,0:T(4,128)(2,1)} %bitcast.8), custom_call_target="tpu_custom_call" | custom-call | tf_op jit(solution)/shard_map/far/pallas_call | solution.py:210
Async XLA Ops:
  0.0 24.1 %copy-start.1 = (s32[384,4]{0,1:T(4,128)S(1)}, s32[384,4]{0,1:T(4,128)}, u32[]{:S(2)}) copy-start(s32[384,4]{0,1:T(4,128)} %param.6) | copy-start | bytes 18436
  2.6 34.9 %all-to-all-start = ((bf16[64,4,1029]{2,1,0:T(4,128)(2,1)}), bf16[64,4,1029]{2,1,0:T(4,128)(2,1)S(1)}, u32[]{:S(2)}, u32[]{:S(2)}) async-start(bf16[64,4,1029]{2,1,0:T(4,128)(2,1)} %get-tuple-element.10), calls=%async_computation | async-start | bytes 1179648 | tf_op jit(solution)/shard_map/all_to_all | solution.py:233
  15.7 4.5 %collective-permute-start = (bf16[16,1029]{1,0:T(8,128)(2,1)}, bf16[16,1029]{1,0:T(8,128)(2,1)S(1)}, u32[]{:S(2)}, u32[]{:S(2)}) collective-permute-start(bf16[16,1029]{1,0:T(8,128)(2,1)} %get-tuple-element.8), channel_id=1, source_target_pairs={{0,64},{64,128},{128,192},{1,65},{65,129},{129,193},{2,66},{66,130... | collective-permute-start | bytes 98792 | tf_op jit(solution)/shard_map/ppermute | solution.py:237
  18.8 5.2 %collective-permute-start.1 = (bf16[16,1029]{1,0:T(8,128)(2,1)}, bf16[16,1029]{1,0:T(8,128)(2,1)S(1)}, u32[]{:S(2)}, u32[]{:S(2)}) collective-permute-start(bf16[16,1029]{1,0:T(8,128)(2,1)} %get-tuple-element.9), channel_id=1, source_target_pairs={{64,0},{128,64},{192,128},{65,1},{129,65},{193,129},{66,2},{130,66... | collective-permute-start | bytes 98792 | tf_op jit(solution)/shard_map/ppermute | solution.py:238
  36.4 1.2 %copy-start = (f32[3,343,384]{2,1,0:T(8,128)}, f32[3,343,384]{2,1,0:T(8,128)S(1)}, u32[]{:S(2)}) copy-start(f32[3,343,384]{2,1,0:T(8,128)S(1)} %near.1.near_hbm) | copy-start | bytes 4741636

commit v2 on v1

--- a/solution.py
+++ b/solution.py
@@ -71,32 +71,28 @@
         spread[comp, t] = y[:, t * LANES:(t + 1) * LANES]
 
 
-def gather_in(spread, picks, comp, dirs, nodes):
-    pieces = [
-        spread[comp, t, pl.ds(d, nodes, stride=dirs), :]
-        for d in range(dirs)
-        for t in range(spread.shape[1])
-    ]
-    moved = jnp.concatenate(pieces, axis=1).astype(jnp.bfloat16)
-    return jnp.dot(moved, picks[...], preferred_element_type=jnp.float32)
-
-
-def near_kernel(m_hbm, low_ref, high_ref, codes_ref, a_hbm, near_hbm, stage, source, picks, spread, held, total, sems, m_sems, out_sems):
-    comps, nodes, nboxes = m_hbm.shape
+def gather_in(total, spread, picks, comp, dirs, nodes):
+    tiles = spread.shape[1]
+    wide = tiles * LANES
+    for d in range(dirs):
+        pieces = [spread[comp, t, pl.ds(d, nodes, stride=dirs), :] for t in range(tiles)]
+        moved = jnp.concatenate(pieces, axis=1).astype(jnp.bfloat16)
+        part = jnp.dot(moved, picks[pl.ds(d * wide, wide), :], preferred_element_type=jnp.float32)
+        total = part if total is None else total + part
+    return total
+
+
+def near_kernel(m_ref, low_ref, high_ref, codes_ref, a_hbm, near_hbm, stage, source, picks, spread, held, total, sems, out_sems):
+    comps, nodes, nboxes = m_ref.shape
     dirs, width = a_hbm.shape[1:]
     wide = picks.shape[0] // dirs
 
     def fetch(comp):
         return pltpu.make_async_copy(a_hbm.at[pl.ds(comp * nodes, nodes)], held.at[comp], sems.at[comp])
 
-    def fetch_m(comp):
-        return pltpu.make_async_copy(m_hbm.at[comp], total.at[comp], m_sems.at[comp])
-
     def store(comp):
         return pltpu.make_async_copy(total.at[comp], near_hbm.at[comp], out_sems.at[comp])
 
-    for comp in range(comps):
-        fetch_m(comp).start()
     for comp in range(comps):
         fetch(comp).start()
     blank = jnp.zeros((wide - nboxes - 2 * FACE, width), jnp.bfloat16)
@@ -109,8 +105,7 @@
         wanted = jnp.where((code < 0) | (code >= nboxes + 2 * FACE), -1, wanted)
         picks[pl.ds(d * wide, wide), :] = (place == wanted).astype(jnp.bfloat16)
     for comp in range(comps):
-        fetch_m(comp).wait()
-        stage[pl.ds(comp * nodes, nodes), :] = total[comp]
+        stage[pl.ds(comp * nodes, nodes), :] = m_ref[comp]
     source[:, :nboxes] = stage[...].astype(jnp.bfloat16)
 
     @pl.loop(0, comps)
@@ -119,13 +114,10 @@
         a = held[comp].reshape(nodes * dirs, width)
         spread_out(jnp.dot(a, source[...], preferred_element_type=jnp.float32), spread, comp)
 
-    @pl.loop(0, comps)
-    def _(comp):
-        total[comp] = gather_in(spread, picks, comp, dirs, nodes)
+    for comp in range(comps):
+        total[comp] = gather_in(None, spread, picks, comp, dirs, nodes)
         store(comp).start()
-
-    @pl.loop(0, comps)
-    def _(comp):
+    for comp in range(comps):
         store(comp).wait()
 
 
@@ -153,23 +145,17 @@
     for d in range(dirs):
         picks[pl.ds(d * wide, wide), :] = (place == codes_ref[pl.ds(d, 1), :]).astype(jnp.bfloat16)
 
-    @pl.loop(0, comps + 1)
-    def _(comp):
-        @pl.when(comp < comps)
-        def _():
-            fetch(comp).wait()
-            a = held[comp].reshape(nodes * dirs, width)
-            spread_out(jnp.dot(a, source[...], preferred_element_type=jnp.float32), spread, comp)
-
-        @pl.when(comp > 0)
-        def _():
-            last = comp - 1
-            fetch_near(last).wait()
-            total[last] = total[last] + gather_in(spread, picks, last, dirs, nodes)
-            store(last).start()
-
     @pl.loop(0, comps)
     def _(comp):
+        fetch(comp).wait()
+        a = held[comp].reshape(nodes * dirs, width)
+        spread_out(jnp.dot(a, source[...], preferred_element_type=jnp.float32), spread, comp)
+
+    for comp in range(comps):
+        fetch_near(comp).wait()
+        total[comp] = gather_in(total[comp], spread, picks, comp, dirs, nodes)
+        store(comp).start()
+    for comp in range(comps):
         store(comp).wait()
 
 
@@ -183,8 +169,8 @@
     wide = nboxes + LANES
     return pl.pallas_call(
         near_kernel,
-        out_shape=jax.ShapeDtypeStruct((comps, nodes, nboxes), jnp.float32),
-        in_specs=[HBM, VMEM, VMEM, VMEM, HBM],
+        out_shape=pltpu.MemorySpace.HBM((comps, nodes, nboxes), jnp.float32),
+        in_specs=[VMEM, VMEM, VMEM, VMEM, HBM],
         out_specs=HBM,
         scratch_shapes=[
             pltpu.VMEM((width, nboxes), jnp.float32),
@@ -193,7 +179,6 @@
             pltpu.VMEM((comps, wide // LANES, nodes * dirs, LANES), jnp.float32),
             pltpu.VMEM((comps, nodes, dirs, width), jnp.bfloat16),
             pltpu.VMEM((comps, nodes, nboxes), jnp.float32),
-            pltpu.SemaphoreType.DMA((comps,)),
             pltpu.SemaphoreType.DMA((comps,)),
             pltpu.SemaphoreType.DMA((comps,)),
         ],

time: 45.6 us -> 43.4 us (0.952)
  local copies, waits for them, and re-layouts: 1.15 us -> 0.01 us
  Pallas kernels: 22.6 us -> 21.6 us
    unnamed x4, local copies, waits for them, and re-layouts: 1.15 us -> 0.01 us
    pallas_call x1, Pallas kernels: 12.3 us -> 11.2 us  [near_sum(): pl.pallas_call(near_kernel, out_shape=pltpu.MemorySpace.HBM((comps, nodes...]
  transfers between devices with their start and end apart: 3 -> 3, of which waited for: 2 -> 2; matrix products, arithmetic and copies ran while one was open for 0% -> 0% of each run, Pallas kernels for 27% -> 26%
where the time goes in v2:
time: 43.4 us; the launch traced here: 43.1 us
  Pallas kernels  21.6 us (50%)
  starting transfers between devices  17.6 us (41%)
  waiting for transfers between devices  3.91 us (9%)
    all_to_all x1, starting transfers between devices, local(): ghost = lax.all_to_all(table, 'owner', 0, 0, tiled=True)  13.1 us
    pallas_call x1, Pallas kernels, near_sum(): pl.pallas_call(near_kernel, out_shape=pltpu.MemorySpace.HBM((comps, nodes...  11.2 us
    pallas_call x1, Pallas kernels, far_sum(): pl.pallas_call(far_kernel, out_shape=jax.ShapeDtypeStruct((comps, nodes,...  7.73 us
    ppermute x1, waiting for transfers between devices, local(): high = lax.ppermute(high, 'leaf', backward)  3.85 us
    ppermute x1, starting transfers between devices, local(): low = lax.ppermute(low, 'leaf', forward)  3.12 us
    pallas_call x1, Pallas kernels, make_table(): pl.pallas_call(table_kernel, out_shape=(jax.ShapeDtypeStruct((owners, cap...  2.67 us
    ppermute x1, starting transfers between devices, local(): high = lax.ppermute(high, 'leaf', backward)  1.29 us
  transfers between devices with their start and end apart: 3, of which 2 were waited for; matrix products, arithmetic and copies ran while one was open for 0% of the time, Pallas kernels for 26%

profile of v2, /device:TPU:1, one launch (start us, length us, event | category | flops | bytes accessed | tf_op | source)
XLA Modules:
  0.0 43.1 jit_solution(12150557648673404966)
XLA Ops:
  0.0 0.0 copy-start
  0.0 0.0 copy-start.1
  0.0 2.7 %table.1 = (bf16[64,4,1029]{2,1,0:T(4,128)(2,1)}, bf16[16,1029]{1,0:T(8,128)(2,1)}, bf16[16,1029]{1,0:T(8,128)(2,1)}) custom-call(f32[3,343,384]{2,1,0:T(8,128)} %m_ref.1, f32[3,343,384]{2,1,0:T(8,128)} %m_ref.1, s32[4,64]{1,0:T(4,128)} %bitcast.9), custom_call_target="tpu_custom_call" | custom-call | tf_op jit(solution)/shard_map/table/pallas_call | solution.py:46
  2.7 13.1 %all-to-all-start = ((bf16[64,4,1029]{2,1,0:T(4,128)(2,1)}), bf16[64,4,1029]{2,1,0:T(4,128)(2,1)S(1)}, u32[]{:S(2)}, u32[]{:S(2)}) async-start(bf16[64,4,1029]{2,1,0:T(4,128)(2,1)} %get-tuple-element.10), calls=%async_computation | async-start | bytes 1179648 | tf_op jit(solution)/shard_map/all_to_all | solution.py:218
  15.8 3.1 %collective-permute-start = (bf16[16,1029]{1,0:T(8,128)(2,1)}, bf16[16,1029]{1,0:T(8,128)(2,1)S(1)}, u32[]{:S(2)}, u32[]{:S(2)}) collective-permute-start(bf16[16,1029]{1,0:T(8,128)(2,1)} %get-tuple-element.8), channel_id=1, source_target_pairs={{0,64},{64,128},{128,192},{1,65},{65,129},{129,193},{2,66},{66,130... | collective-permute-start | bytes 98792 | tf_op jit(solution)/shard_map/ppermute | solution.py:222
  19.0 1.3 %collective-permute-start.1 = (bf16[16,1029]{1,0:T(8,128)(2,1)}, bf16[16,1029]{1,0:T(8,128)(2,1)S(1)}, u32[]{:S(2)}, u32[]{:S(2)}) collective-permute-start(bf16[16,1029]{1,0:T(8,128)(2,1)} %get-tuple-element.9), channel_id=1, source_target_pairs={{64,0},{128,64},{192,128},{65,1},{129,65},{193,129},{66,2},{130,66... | collective-permute-start | bytes 98792 | tf_op jit(solution)/shard_map/ppermute | solution.py:223
  20.3 0.1 collective-permute-done.low_ref
  20.3 3.8 %collective-permute-done.1.high_ref = bf16[16,1029]{1,0:T(8,128)(2,1)S(1)} collective-permute-done((bf16[16,1029]{1,0:T(8,128)(2,1)}, bf16[16,1029]{1,0:T(8,128)(2,1)S(1)}, u32[]{:S(2)}, u32[]{:S(2)}) %collective-permute-start.1) | collective-permute-done | bytes 32960 | tf_op jit(solution)/shard_map/ppermute | solution.py:223
  24.2 0.0 copy-done
  24.2 0.0 copy-done.1
  24.2 11.2 %near.1.near_hbm = f32[3,343,384]{2,1,0:T(8,128)} custom-call(f32[3,343,384]{2,1,0:T(8,128)S(1)} %copy-done, bf16[16,1029]{1,0:T(8,128)(2,1)S(1)} %collective-permute-done.low_ref, bf16[16,1029]{1,0:T(8,128)(2,1)S(1)} %collective-permute-done.1.high_ref, s32[4,384]{1,0:T(4,128)S(1)} %bitcast.5, bf16[1029,4,1029]{2,1,0:T(4,128)(2,1)} %bitcast.7), custom_call_target="tpu_custom_call" | custom-call | tf_op jit(solution)/shard_map/near/pallas_call | solution.py:170
  35.3 0.0 all-to-all-done.g_ref
  35.3 7.7 %far.1 = f32[3,343,384]{2,1,0:T(8,128)} custom-call(f32[3,343,384]{2,1,0:T(8,128)} %near.1.near_hbm, bf16[64,4,1029]{2,1,0:T(4,128)(2,1)S(1)} %all-to-all-done.g_ref, s32[4,384]{1,0:T(4,128)S(1)} %bitcast.6, bf16[1029,4,1029]{2,1,0:T(4,128)(2,1)} %bitcast.8), custom_call_target="tpu_custom_call" | custom-call | tf_op jit(solution)/shard_map/far/pallas_call | solution.py:195
Async XLA Ops:
  0.0 24.2 %copy-start = (f32[3,343,384]{2,1,0:T(8,128)S(1)}, f32[3,343,384]{2,1,0:T(8,128)}, u32[]{:S(2)}) copy-start(f32[3,343,384]{2,1,0:T(8,128)} %m_ref.1) | copy-start | bytes 4741636
  0.0 24.2 %copy-start.1 = (s32[384,4]{0,1:T(4,128)S(1)}, s32[384,4]{0,1:T(4,128)}, u32[]{:S(2)}) copy-start(s32[384,4]{0,1:T(4,128)} %param.6) | copy-start | bytes 18436
  2.7 32.7 %all-to-all-start = ((bf16[64,4,1029]{2,1,0:T(4,128)(2,1)}), bf16[64,4,1029]{2,1,0:T(4,128)(2,1)S(1)}, u32[]{:S(2)}, u32[]{:S(2)}) async-start(bf16[64,4,1029]{2,1,0:T(4,128)(2,1)} %get-tuple-element.10), calls=%async_computation | async-start | bytes 1179648 | tf_op jit(solution)/shard_map/all_to_all | solution.py:218
  15.8 4.5 %collective-permute-start = (bf16[16,1029]{1,0:T(8,128)(2,1)}, bf16[16,1029]{1,0:T(8,128)(2,1)S(1)}, u32[]{:S(2)}, u32[]{:S(2)}) collective-permute-start(bf16[16,1029]{1,0:T(8,128)(2,1)} %get-tuple-element.8), channel_id=1, source_target_pairs={{0,64},{64,128},{128,192},{1,65},{65,129},{129,193},{2,66},{66,130... | collective-permute-start | bytes 98792 | tf_op jit(solution)/shard_map/ppermute | solution.py:222
  19.0 5.2 %collective-permute-start.1 = (bf16[16,1029]{1,0:T(8,128)(2,1)}, bf16[16,1029]{1,0:T(8,128)(2,1)S(1)}, u32[]{:S(2)}, u32[]{:S(2)}) collective-permute-start(bf16[16,1029]{1,0:T(8,128)(2,1)} %get-tuple-element.9), channel_id=1, source_target_pairs={{64,0},{128,64},{192,128},{65,1},{129,65},{193,129},{66,2},{130,66... | collective-permute-start | bytes 98792 | tf_op jit(solution)/shard_map/ppermute | solution.py:223

commit v3 on v2

--- a/solution.py
+++ b/solution.py
@@ -82,19 +82,20 @@
     return total
 
 
-def near_kernel(m_ref, low_ref, high_ref, codes_ref, a_hbm, near_hbm, stage, source, picks, spread, held, total, sems, out_sems):
+def load_kernel(a_hbm, a_ref, sem):
+    copy = pltpu.make_async_copy(a_hbm, a_ref, sem)
+    copy.start()
+    copy.wait()
+
+
+def near_kernel(m_ref, low_ref, high_ref, codes_ref, a_ref, near_hbm, stage, source, picks, spread, total, out_sems):
     comps, nodes, nboxes = m_ref.shape
-    dirs, width = a_hbm.shape[1:]
+    dirs, width = a_ref.shape[1:]
     wide = picks.shape[0] // dirs
-
-    def fetch(comp):
-        return pltpu.make_async_copy(a_hbm.at[pl.ds(comp * nodes, nodes)], held.at[comp], sems.at[comp])
 
     def store(comp):
         return pltpu.make_async_copy(total.at[comp], near_hbm.at[comp], out_sems.at[comp])
 
-    for comp in range(comps):
-        fetch(comp).start()
     blank = jnp.zeros((wide - nboxes - 2 * FACE, width), jnp.bfloat16)
     source[:, nboxes:] = jnp.concatenate([low_ref[...], high_ref[...], blank], axis=0).T
     place = lax.broadcasted_iota(jnp.int32, (wide, nboxes), 0)
@@ -110,8 +111,7 @@
 
     @pl.loop(0, comps)
     def _(comp):
-        fetch(comp).wait()
-        a = held[comp].reshape(nodes * dirs, width)
+        a = a_ref[pl.ds(comp * nodes, nodes)].reshape(nodes * dirs, width)
         spread_out(jnp.dot(a, source[...], preferred_element_type=jnp.float32), spread, comp)
 
     for comp in range(comps):
@@ -167,22 +167,29 @@
     comps, nodes, nboxes = multipoles.shape
     width, dirs, _ = rows.shape
     wide = nboxes + LANES
+    rows = pl.pallas_call(
+        load_kernel,
+        out_shape=jax.ShapeDtypeStruct(rows.shape, rows.dtype),
+        in_specs=[HBM],
+        out_specs=VMEM,
+        scratch_shapes=[pltpu.SemaphoreType.DMA],
+        compiler_params=pltpu.CompilerParams(vmem_limit_bytes=45_000_000),
+        name="load",
+    )(rows)
     return pl.pallas_call(
         near_kernel,
         out_shape=pltpu.MemorySpace.HBM((comps, nodes, nboxes), jnp.float32),
-        in_specs=[VMEM, VMEM, VMEM, VMEM, HBM],
+        in_specs=[VMEM, VMEM, VMEM, VMEM, VMEM],
         out_specs=HBM,
         scratch_shapes=[
             pltpu.VMEM((width, nboxes), jnp.float32),
             pltpu.VMEM((width, wide), jnp.bfloat16),
             pltpu.VMEM((dirs * wide, nboxes), jnp.bfloat16),
             pltpu.VMEM((comps, wide // LANES, nodes * dirs, LANES), jnp.float32),
-            pltpu.VMEM((comps, nodes, dirs, width), jnp.bfloat16),
             pltpu.VMEM((comps, nodes, nboxes), jnp.float32),
             pltpu.SemaphoreType.DMA((comps,)),
-            pltpu.SemaphoreType.DMA((comps,)),
         ],
-        compiler_params=pltpu.CompilerParams(vmem_limit_bytes=52 << 20),
+        compiler_params=pltpu.CompilerParams(vmem_limit_bytes=30 << 20),
         name="near",
     )(multipoles, low, high, codes, rows)
 

time: 43.4 us -> 42.8 us (0.986)
  waiting for transfers between devices: 3.91 us -> 0.38 us
  Pallas kernels: 21.6 us -> 24.2 us
    pallas_call x0 -> x1, Pallas kernels: none -> 3.82 us  [near_sum(): pl.pallas_call(load_kernel, out_shape=jax.ShapeDtypeStruct(rows.shape, ro...]
    ppermute x1, waiting for transfers between devices: 3.85 us -> 0.04 us  [local(): high = lax.ppermute(high, 'leaf', backward)]
    pallas_call x1, Pallas kernels: 11.2 us -> 10.1 us  [near_sum(): pl.pallas_call(near_kernel, out_shape=pltpu.MemorySpace.HBM((comps, nodes...]
  transfers between devices with their start and end apart: 3 -> 3, of which waited for: 2 -> 1; matrix products, arithmetic and copies ran while one was open for 0% -> 0% of each run, Pallas kernels for 26% -> 33%
where the time goes in v3:
time: 42.8 us; the launch traced here: 42.4 us
  Pallas kernels  24.2 us (57%)
  starting transfers between devices  17.6 us (41%)
    all_to_all x1, starting transfers between devices, local(): ghost = lax.all_to_all(table, 'owner', 0, 0, tiled=True)  13.1 us
    pallas_call x1, Pallas kernels, near_sum(): pl.pallas_call(near_kernel, out_shape=pltpu.MemorySpace.HBM((comps, nodes...  10.1 us
    pallas_call x1, Pallas kernels, far_sum(): pl.pallas_call(far_kernel, out_shape=jax.ShapeDtypeStruct((comps, nodes,...  7.72 us
    pallas_call x1, Pallas kernels, near_sum(): pl.pallas_call(load_kernel, out_shape=jax.ShapeDtypeStruct(rows.shape, ro...  3.82 us
    ppermute x1, starting transfers between devices, local(): low = lax.ppermute(low, 'leaf', forward)  3.11 us
    pallas_call x1, Pallas kernels, make_table(): pl.pallas_call(table_kernel, out_shape=(jax.ShapeDtypeStruct((owners, cap...  2.55 us
    ppermute x1, starting transfers between devices, local(): high = lax.ppermute(high, 'leaf', backward)  1.29 us
  transfers between devices with their start and end apart: 3, of which 1 were waited for; matrix products, arithmetic and copies ran while one was open for 0% of the time, Pallas kernels for 33%

profile of v3, /device:TPU:1, one launch (start us, length us, event | category | flops | bytes accessed | tf_op | source)
XLA Modules:
  0.0 42.4 jit_solution(3268452176621333672)
XLA Ops:
  0.0 2.5 %table.1 = (bf16[64,4,1029]{2,1,0:T(4,128)(2,1)}, bf16[16,1029]{1,0:T(8,128)(2,1)}, bf16[16,1029]{1,0:T(8,128)(2,1)}) custom-call(f32[3,343,384]{2,1,0:T(8,128)} %m_ref.1, f32[3,343,384]{2,1,0:T(8,128)} %m_ref.1, s32[4,64]{1,0:T(4,128)} %bitcast.9), custom_call_target="tpu_custom_call" | custom-call | tf_op jit(solution)/shard_map/table/pallas_call | solution.py:46
  2.6 13.1 %all-to-all-start = ((bf16[64,4,1029]{2,1,0:T(4,128)(2,1)}), bf16[64,4,1029]{2,1,0:T(4,128)(2,1)S(1)}, u32[]{:S(2)}, u32[]{:S(2)}) async-start(bf16[64,4,1029]{2,1,0:T(4,128)(2,1)} %get-tuple-element.10), calls=%async_computation | async-start | bytes 1179648 | tf_op jit(solution)/shard_map/all_to_all | solution.py:225
  15.7 3.1 %collective-permute-start = (bf16[16,1029]{1,0:T(8,128)(2,1)}, bf16[16,1029]{1,0:T(8,128)(2,1)S(1)}, u32[]{:S(2)}, u32[]{:S(2)}) collective-permute-start(bf16[16,1029]{1,0:T(8,128)(2,1)} %get-tuple-element.8), channel_id=1, source_target_pairs={{0,64},{64,128},{128,192},{1,65},{65,129},{129,193},{2,66},{66,130... | collective-permute-start | bytes 98792 | tf_op jit(solution)/shard_map/ppermute | solution.py:229
  18.8 1.3 %collective-permute-start.1 = (bf16[16,1029]{1,0:T(8,128)(2,1)}, bf16[16,1029]{1,0:T(8,128)(2,1)S(1)}, u32[]{:S(2)}, u32[]{:S(2)}) collective-permute-start(bf16[16,1029]{1,0:T(8,128)(2,1)} %get-tuple-element.9), channel_id=1, source_target_pairs={{64,0},{128,64},{192,128},{65,1},{129,65},{193,129},{66,2},{130,66... | collective-permute-start | bytes 98792 | tf_op jit(solution)/shard_map/ppermute | solution.py:230
  20.1 0.0 copy-start
  20.1 0.0 copy-start.1
  20.2 3.8 %load.1.a_ref = bf16[1029,4,1029]{2,1,0:T(4,128)(2,1)S(1)} custom-call(bf16[1029,4,1029]{2,1,0:T(4,128)(2,1)} %bitcast.7), custom_call_target="tpu_custom_call" | custom-call | tf_op jit(solution)/shard_map/load/pallas_call | solution.py:170
  24.0 0.0 collective-permute-done.low_ref
  24.0 0.0 collective-permute-done.1.high_ref
  24.0 0.2 copy-done
  24.2 0.0 copy-done.1
  24.2 10.1 %near.1.near_hbm = f32[3,343,384]{2,1,0:T(8,128)} custom-call(f32[3,343,384]{2,1,0:T(8,128)S(1)} %copy-done, bf16[16,1029]{1,0:T(8,128)(2,1)S(1)} %collective-permute-done.low_ref, bf16[16,1029]{1,0:T(8,128)(2,1)S(1)} %collective-permute-done.1.high_ref, s32[4,384]{1,0:T(4,128)S(1)} %bitcast.5, bf16[1029,4,1029]{2,1,0:T(4,128)(2,1)S(1)} %load.1.a_ref), custom_call_target="tpu_custom_call" | custom-call | tf_op jit(solution)/shard_map/near/pallas_call | solution.py:179
  34.4 0.3 all-to-all-done.g_ref
  34.7 7.7 %far.1 = f32[3,343,384]{2,1,0:T(8,128)} custom-call(f32[3,343,384]{2,1,0:T(8,128)} %near.1.near_hbm, bf16[64,4,1029]{2,1,0:T(4,128)(2,1)S(1)} %all-to-all-done.g_ref, s32[4,384]{1,0:T(4,128)S(1)} %bitcast.6, bf16[1029,4,1029]{2,1,0:T(4,128)(2,1)} %bitcast.8), custom_call_target="tpu_custom_call" | custom-call | tf_op jit(solution)/shard_map/far/pallas_call | solution.py:202
Async XLA Ops:
  2.6 32.2 %all-to-all-start = ((bf16[64,4,1029]{2,1,0:T(4,128)(2,1)}), bf16[64,4,1029]{2,1,0:T(4,128)(2,1)S(1)}, u32[]{:S(2)}, u32[]{:S(2)}) async-start(bf16[64,4,1029]{2,1,0:T(4,128)(2,1)} %get-tuple-element.10), calls=%async_computation | async-start | bytes 1179648 | tf_op jit(solution)/shard_map/all_to_all | solution.py:225
  15.7 8.3 %collective-permute-start = (bf16[16,1029]{1,0:T(8,128)(2,1)}, bf16[16,1029]{1,0:T(8,128)(2,1)S(1)}, u32[]{:S(2)}, u32[]{:S(2)}) collective-permute-start(bf16[16,1029]{1,0:T(8,128)(2,1)} %get-tuple-element.8), channel_id=1, source_target_pairs={{0,64},{64,128},{128,192},{1,65},{65,129},{129,193},{2,66},{66,130... | collective-permute-start | bytes 98792 | tf_op jit(solution)/shard_map/ppermute | solution.py:229
  18.8 5.2 %collective-permute-start.1 = (bf16[16,1029]{1,0:T(8,128)(2,1)}, bf16[16,1029]{1,0:T(8,128)(2,1)S(1)}, u32[]{:S(2)}, u32[]{:S(2)}) collective-permute-start(bf16[16,1029]{1,0:T(8,128)(2,1)} %get-tuple-element.9), channel_id=1, source_target_pairs={{64,0},{128,64},{192,128},{65,1},{129,65},{193,129},{66,2},{130,66... | collective-permute-start | bytes 98792 | tf_op jit(solution)/shard_map/ppermute | solution.py:230
  20.1 4.1 %copy-start = (f32[3,343,384]{2,1,0:T(8,128)S(1)}, f32[3,343,384]{2,1,0:T(8,128)}, u32[]{:S(2)}) copy-start(f32[3,343,384]{2,1,0:T(8,128)} %m_ref.1) | copy-start | bytes 4741636
  20.1 4.1 %copy-start.1 = (s32[384,4]{0,1:T(4,128)S(1)}, s32[384,4]{0,1:T(4,128)}, u32[]{:S(2)}) copy-start(s32[384,4]{0,1:T(4,128)} %param.6) | copy-start | bytes 18436

commit v4 on v2

--- a/solution.py
+++ b/solution.py
@@ -82,31 +82,113 @@
     return total
 
 
-def near_kernel(m_ref, low_ref, high_ref, codes_ref, a_hbm, near_hbm, stage, source, picks, spread, held, total, sems, out_sems):
-    comps, nodes, nboxes = m_ref.shape
+def stack(stage, block):
+    comps, nodes, _ = block.shape
+    for comp in range(comps):
+        stage[pl.ds(comp * nodes, nodes), :] = block[comp]
+    return stage[...].astype(jnp.bfloat16)
+
+
+def own_kernel(m_hbm, codes_ref, a_hbm, part_hbm, a_ref, block, stage, source, picks, spread, total, m_sem, sems, out_sems):
+    comps, nodes, nboxes = total.shape
     dirs, width = a_hbm.shape[1:]
-    wide = picks.shape[0] // dirs
+    wide = source.shape[1]
 
     def fetch(comp):
-        return pltpu.make_async_copy(a_hbm.at[pl.ds(comp * nodes, nodes)], held.at[comp], sems.at[comp])
+        rows = pl.ds(comp * nodes, nodes)
+        return pltpu.make_async_copy(a_hbm.at[rows], a_ref.at[rows], sems.at[comp])
+
+    def store(comp):
+        return pltpu.make_async_copy(total.at[comp], part_hbm.at[comp], out_sems.at[comp])
+
+    load = pltpu.make_async_copy(m_hbm.at[:, :, :wide], block, m_sem)
+    load.start()
+    for comp in range(comps):
+        fetch(comp).start()
+    place = lax.broadcasted_iota(jnp.int32, (wide, nboxes), 0) + FACE
+    for d in range(dirs):
+        picks[pl.ds(d * wide, wide), :] = (place == codes_ref[pl.ds(d, 1), :]).astype(jnp.bfloat16)
+    load.wait()
+    source[...] = stack(stage, block)
+
+    @pl.loop(0, comps)
+    def _(comp):
+        fetch(comp).wait()
+        a = a_ref[pl.ds(comp * nodes, nodes)].reshape(nodes * dirs, width)
+        spread_out(jnp.dot(a, source[...], preferred_element_type=jnp.float32), spread, comp)
+
+    for comp in range(comps):
+        total[comp] = gather_in(None, spread, picks, comp, dirs, nodes)
+        store(comp).start()
+    for comp in range(comps):
+        store(comp).wait()
+
+
+def rim_kernel(part_hbm, m_hbm, low_ref, high_ref, codes_ref, a_ref, near_hbm, block, stage, source, picks, spread, total, m_sem, sems, out_sems):
+    comps, nodes, nboxes = total.shape
+    dirs, width = a_ref.shape[1:]
+    wide = source.shape[1]
+    tail = block.shape[2]
+    first = nboxes - tail
+
+    def fetch(comp):
+        return pltpu.make_async_copy(part_hbm.at[comp], total.at[comp], sems.at[comp])
 
     def store(comp):
         return pltpu.make_async_copy(total.at[comp], near_hbm.at[comp], out_sems.at[comp])
 
+    load = pltpu.make_async_copy(m_hbm.at[:, :, first:], block, m_sem)
+    load.start()
     for comp in range(comps):
         fetch(comp).start()
-    blank = jnp.zeros((wide - nboxes - 2 * FACE, width), jnp.bfloat16)
-    source[:, nboxes:] = jnp.concatenate([low_ref[...], high_ref[...], blank], axis=0).T
+    blank = jnp.zeros((wide - tail - 2 * FACE, width), jnp.bfloat16)
+    source[:, tail:] = jnp.concatenate([low_ref[...], high_ref[...], blank], axis=0).T
     place = lax.broadcasted_iota(jnp.int32, (wide, nboxes), 0)
     for d in range(dirs):
         code = codes_ref[pl.ds(d, 1), :]
-        low = jnp.where(code < FACE, code + nboxes, code - FACE)
-        wanted = jnp.where(code < nboxes + FACE, low, code)
+        inner = jnp.where(code < nboxes + FACE, code - (first + FACE), code - first)
+        wanted = jnp.where(code < FACE, code + tail, inner)
         wanted = jnp.where((code < 0) | (code >= nboxes + 2 * FACE), -1, wanted)
         picks[pl.ds(d * wide, wide), :] = (place == wanted).astype(jnp.bfloat16)
-    for comp in range(comps):
-        stage[pl.ds(comp * nodes, nodes), :] = m_ref[comp]
-    source[:, :nboxes] = stage[...].astype(jnp.bfloat16)
+    load.wait()
+    source[:, :tail] = stack(stage, block)
+
+    @pl.loop(0, comps)
+    def _(comp):
+        a = a_ref[pl.ds(comp * nodes, nodes)].reshape(nodes * dirs, width)
+        spread_out(jnp.dot(a, source[...], preferred_element_type=jnp.float32), spread, comp)
+
+    for comp in range(comps):
+        fetch(comp).wait()
+        total[comp] = gather_in(total[comp], spread, picks, comp, dirs, nodes)
+        store(comp).start()
+    for comp in range(comps):
+        store(comp).wait()
+
+
+def far_kernel(near_hbm, g_ref, codes_ref, a_hbm, out_hbm, source, picks, spread, held, total, sems, near_sems, out_sems):
+    comps, nodes, nboxes = near_hbm.shape
+    dirs = a_hbm.shape[1]
+    width = a_hbm.shape[2]
+    wide = picks.shape[0] // dirs
+
+    def fetch(comp):
+        return pltpu.make_async_copy(a_hbm.at[pl.ds(comp * nodes, nodes)], held.at[comp], sems.at[comp])
+
+    def fetch_near(comp):
+        return pltpu.make_async_copy(near_hbm.at[comp], total.at[comp], near_sems.at[comp])
+
+    def store(comp):
+        return pltpu.make_async_copy(total.at[comp], out_hbm.at[comp], out_sems.at[comp])
+
+    for comp in range(comps):
+        fetch(comp).start()
+    for comp in range(comps):
+        fetch_near(comp).start()
+    source[...] = g_ref[...].reshape(source.shape[1], source.shape[0]).T
+    place = lax.broadcasted_iota(jnp.int32, (wide, nboxes), 0) + (nboxes + 2 * FACE)
+    for d in range(dirs):
+        picks[pl.ds(d * wide, wide), :] = (place == codes_ref[pl.ds(d, 1), :]).astype(jnp.bfloat16)
 
     @pl.loop(0, comps)
     def _(comp):
@@ -115,43 +197,6 @@
         spread_out(jnp.dot(a, source[...], preferred_element_type=jnp.float32), spread, comp)
 
     for comp in range(comps):
-        total[comp] = gather_in(None, spread, picks, comp, dirs, nodes)
-        store(comp).start()
-    for comp in range(comps):
-        store(comp).wait()
-
-
-def far_kernel(near_hbm, g_ref, codes_ref, a_hbm, out_hbm, source, picks, spread, held, total, sems, near_sems, out_sems):
-    comps, nodes, nboxes = near_hbm.shape
-    dirs = a_hbm.shape[1]
-    width = a_hbm.shape[2]
-    wide = picks.shape[0] // dirs
-
-    def fetch(comp):
-        return pltpu.make_async_copy(a_hbm.at[pl.ds(comp * nodes, nodes)], held.at[comp], sems.at[comp])
-
-    def fetch_near(comp):
-        return pltpu.make_async_copy(near_hbm.at[comp], total.at[comp], near_sems.at[comp])
-
-    def store(comp):
-        return pltpu.make_async_copy(total.at[comp], out_hbm.at[comp], out_sems.at[comp])
-
-    for comp in range(comps):
-        fetch(comp).start()
-    for comp in range(comps):
-        fetch_near(comp).start()
-    source[...] = g_ref[...].reshape(source.shape[1], source.shape[0]).T
-    place = lax.broadcasted_iota(jnp.int32, (wide, nboxes), 0) + (nboxes + 2 * FACE)
-    for d in range(dirs):
-        picks[pl.ds(d * wide, wide), :] = (place == codes_ref[pl.ds(d, 1), :]).astype(jnp.bfloat16)
-
-    @pl.loop(0, comps)
-    def _(comp):
-        fetch(comp).wait()
-        a = held[comp].reshape(nodes * dirs, width)
-        spread_out(jnp.dot(a, source[...], preferred_element_type=jnp.float32), spread, comp)
-
-    for comp in range(comps):
         fetch_near(comp).wait()
         total[comp] = gather_in(total[comp], spread, picks, comp, dirs, nodes)
         store(comp).start()
@@ -164,27 +209,46 @@
 
 
 def near_sum(multipoles, low, high, codes, rows):
-    comps, nodes, nboxes = multipoles.shape
+    shape = multipoles.shape
+    comps, nodes, nboxes = shape
     width, dirs, _ = rows.shape
-    wide = nboxes + LANES
-    return pl.pallas_call(
-        near_kernel,
-        out_shape=pltpu.MemorySpace.HBM((comps, nodes, nboxes), jnp.float32),
-        in_specs=[VMEM, VMEM, VMEM, VMEM, HBM],
-        out_specs=HBM,
-        scratch_shapes=[
-            pltpu.VMEM((width, nboxes), jnp.float32),
+    wide = 2 * LANES
+    tail = nboxes - wide
+
+    def scratch(lanes):
+        return [
+            pltpu.VMEM((comps, nodes, lanes), jnp.float32),
+            pltpu.VMEM((width, lanes), jnp.float32),
             pltpu.VMEM((width, wide), jnp.bfloat16),
             pltpu.VMEM((dirs * wide, nboxes), jnp.bfloat16),
             pltpu.VMEM((comps, wide // LANES, nodes * dirs, LANES), jnp.float32),
-            pltpu.VMEM((comps, nodes, dirs, width), jnp.bfloat16),
-            pltpu.VMEM((comps, nodes, nboxes), jnp.float32),
-            pltpu.SemaphoreType.DMA((comps,)),
-            pltpu.SemaphoreType.DMA((comps,)),
-        ],
-        compiler_params=pltpu.CompilerParams(vmem_limit_bytes=52 << 20),
-        name="near",
-    )(multipoles, low, high, codes, rows)
+            pltpu.VMEM(shape, jnp.float32),
+            pltpu.SemaphoreType.DMA,
+            pltpu.SemaphoreType.DMA((comps,)),
+            pltpu.SemaphoreType.DMA((comps,)),
+        ]
+
+    part, rows = pl.pallas_call(
+        own_kernel,
+        out_shape=(
+            jax.ShapeDtypeStruct(shape, jnp.float32),
+            jax.ShapeDtypeStruct(rows.shape, rows.dtype),
+        ),
+        in_specs=[HBM, VMEM, HBM],
+        out_specs=(HBM, VMEM),
+        scratch_shapes=scratch(wide),
+        compiler_params=pltpu.CompilerParams(vmem_limit_bytes=42_000_000),
+        name="own",
+    )(multipoles, codes, rows)
+    return pl.pallas_call(
+        rim_kernel,
+        out_shape=pltpu.MemorySpace.HBM(shape, jnp.float32),
+        in_specs=[HBM, HBM, VMEM, VMEM, VMEM, VMEM],
+        out_specs=HBM,
+        scratch_shapes=scratch(tail),
+        compiler_params=pltpu.CompilerParams(vmem_limit_bytes=30 << 20),
+        name="rim",
+    )(part, multipoles, low, high, codes, rows)
 
 
 def far_sum(near, ghost, codes, rows):

time: 43.4 us -> 42.8 us (0.986)
  waiting for transfers between devices: 3.91 us -> 1.09 us
  Pallas kernels: 21.6 us -> 23.8 us
    ppermute x1, waiting for transfers between devices: 3.85 us -> 0.01 us  [local(): high = lax.ppermute(high, 'leaf', backward)]
    pallas_call x1 -> x2, Pallas kernels: 11.2 us -> 13.4 us  [the longest x1 7.04 us: near_sum(): pl.pallas_call(own_kernel, out_shape=(jax.ShapeDtypeStruct(shape, jnp.flo...]
    all_to_all x1, waiting for transfers between devices: 0.01 us -> 1.09 us  [local(): ghost = lax.all_to_all(table, 'owner', 0, 0, tiled=True)]
  transfers between devices with their start and end apart: 3 -> 3, of which waited for: 2 -> 1; matrix products, arithmetic and copies ran while one was open for 0% -> 0% of each run, Pallas kernels for 26% -> 32%
where the time goes in v4:
time: 42.8 us; the launch traced here: 42.6 us
  Pallas kernels  23.8 us (56%)
  starting transfers between devices  17.6 us (41%)
  waiting for transfers between devices  1.09 us (3%)
    all_to_all x1, starting transfers between devices, local(): ghost = lax.all_to_all(table, 'owner', 0, 0, tiled=True)  13.1 us
    pallas_call x1, Pallas kernels, far_sum(): pl.pallas_call(far_kernel, out_shape=jax.ShapeDtypeStruct((comps, nodes,...  7.73 us
    pallas_call x1, Pallas kernels, near_sum(): pl.pallas_call(own_kernel, out_shape=(jax.ShapeDtypeStruct(shape, jnp.flo...  7.04 us
    pallas_call x1, Pallas kernels, near_sum(): pl.pallas_call(rim_kernel, out_shape=pltpu.MemorySpace.HBM(shape, jnp.flo...  6.41 us
    ppermute x1, starting transfers between devices, local(): low = lax.ppermute(low, 'leaf', forward)  3.12 us
    pallas_call x1, Pallas kernels, make_table(): pl.pallas_call(table_kernel, out_shape=(jax.ShapeDtypeStruct((owners, cap...  2.68 us
    ppermute x1, starting transfers between devices, local(): high = lax.ppermute(high, 'leaf', backward)  1.29 us
    all_to_all x1, waiting for transfers between devices, local(): ghost = lax.all_to_all(table, 'owner', 0, 0, tiled=True)  1.09 us
  transfers between devices with their start and end apart: 3, of which 1 were waited for; matrix products, arithmetic and copies ran while one was open for 0% of the time, Pallas kernels for 32%

profile of v4, /device:TPU:1, one launch (start us, length us, event | category | flops | bytes accessed | tf_op | source)
XLA Modules:
  0.0 42.6 jit_solution(15560325383564587436)
XLA Ops:
  0.0 0.0 copy-start
  0.0 0.0 copy-start.1
  0.0 2.7 %table.1 = (bf16[64,4,1029]{2,1,0:T(4,128)(2,1)}, bf16[16,1029]{1,0:T(8,128)(2,1)}, bf16[16,1029]{1,0:T(8,128)(2,1)}) custom-call(f32[3,343,384]{2,1,0:T(8,128)} %m_hbm.3, f32[3,343,384]{2,1,0:T(8,128)} %m_hbm.3, s32[4,64]{1,0:T(4,128)} %bitcast.10), custom_call_target="tpu_custom_call" | custom-call | tf_op jit(solution)/shard_map/table/pallas_call | solution.py:46
  2.7 13.1 %all-to-all-start = ((bf16[64,4,1029]{2,1,0:T(4,128)(2,1)}), bf16[64,4,1029]{2,1,0:T(4,128)(2,1)S(1)}, u32[]{:S(2)}, u32[]{:S(2)}) async-start(bf16[64,4,1029]{2,1,0:T(4,128)(2,1)} %get-tuple-element.14), calls=%async_computation | async-start | bytes 1179648 | tf_op jit(solution)/shard_map/all_to_all | solution.py:282
  15.8 3.1 %collective-permute-start = (bf16[16,1029]{1,0:T(8,128)(2,1)}, bf16[16,1029]{1,0:T(8,128)(2,1)S(1)}, u32[]{:S(2)}, u32[]{:S(2)}) collective-permute-start(bf16[16,1029]{1,0:T(8,128)(2,1)} %get-tuple-element.11), channel_id=1, source_target_pairs={{0,64},{64,128},{128,192},{1,65},{65,129},{129,193},{2,66},{66,130... | collective-permute-start | bytes 98792 | tf_op jit(solution)/shard_map/ppermute | solution.py:286
  19.0 1.3 %collective-permute-start.1 = (bf16[16,1029]{1,0:T(8,128)(2,1)}, bf16[16,1029]{1,0:T(8,128)(2,1)S(1)}, u32[]{:S(2)}, u32[]{:S(2)}) collective-permute-start(bf16[16,1029]{1,0:T(8,128)(2,1)} %get-tuple-element.12), channel_id=1, source_target_pairs={{64,0},{128,64},{192,128},{65,1},{129,65},{193,129},{66,2},{130,66... | collective-permute-start | bytes 98792 | tf_op jit(solution)/shard_map/ppermute | solution.py:287
  20.3 0.0 copy-done
  20.3 0.0 copy-done.1
  20.3 7.0 %own.1 = (f32[3,343,384]{2,1,0:T(8,128)S(1)}, bf16[1029,4,1029]{2,1,0:T(4,128)(2,1)S(1)}) custom-call(f32[3,343,384]{2,1,0:T(8,128)S(1)} %copy-done, s32[4,384]{1,0:T(4,128)S(1)} %bitcast.5, bf16[1029,4,1029]{2,1,0:T(4,128)(2,1)} %bitcast.8), custom_call_target="tpu_custom_call" | custom-call | tf_op jit(solution)/shard_map/own/pallas_call | solution.py:231
  27.3 0.0 collective-permute-done.low_ref
  27.3 0.0 collective-permute-done.1.high_ref
  27.4 6.4 %rim.1.near_hbm = f32[3,343,384]{2,1,0:T(8,128)} custom-call(f32[3,343,384]{2,1,0:T(8,128)S(1)} %get-tuple-element.10.part_hbm, f32[3,343,384]{2,1,0:T(8,128)S(1)} %copy-done, bf16[16,1029]{1,0:T(8,128)(2,1)S(1)} %collective-permute-done.low_ref, bf16[16,1029]{1,0:T(8,128)(2,1)S(1)} %collective-permute-done.1.high_ref, s32[4,384]{1,0:T(4,128)S(1)} %bitcast.6, ...), custom_call_target="tpu_custom_call" | custom-call | tf_op jit(solution)/shard_map/rim/pallas_call | solution.py:243
  33.8 1.1 %all-to-all-done.g_ref = bf16[64,4,1029]{2,1,0:T(4,128)(2,1)S(1)} async-done(((bf16[64,4,1029]{2,1,0:T(4,128)(2,1)}), bf16[64,4,1029]{2,1,0:T(4,128)(2,1)S(1)}, u32[]{:S(2)}, u32[]{:S(2)}) %all-to-all-start) | async-done | bytes 526880 | tf_op jit(solution)/shard_map/all_to_all | solution.py:282
  34.9 7.7 %far.1 = f32[3,343,384]{2,1,0:T(8,128)} custom-call(f32[3,343,384]{2,1,0:T(8,128)} %rim.1.near_hbm, bf16[64,4,1029]{2,1,0:T(4,128)(2,1)S(1)} %all-to-all-done.g_ref, s32[4,384]{1,0:T(4,128)S(1)} %bitcast.7, bf16[1029,4,1029]{2,1,0:T(4,128)(2,1)} %bitcast.9), custom_call_target="tpu_custom_call" | custom-call | tf_op jit(solution)/shard_map/far/pallas_call | solution.py:259
Async XLA Ops:
  0.0 20.3 %copy-start = (f32[3,343,384]{2,1,0:T(8,128)S(1)}, f32[3,343,384]{2,1,0:T(8,128)}, u32[]{:S(2)}) copy-start(f32[3,343,384]{2,1,0:T(8,128)} %m_hbm.3) | copy-start | bytes 4741636
  0.0 20.3 %copy-start.1 = (s32[384,4]{0,1:T(4,128)S(1)}, s32[384,4]{0,1:T(4,128)}, u32[]{:S(2)}) copy-start(s32[384,4]{0,1:T(4,128)} %param.6) | copy-start | bytes 18436
  2.7 32.2 %all-to-all-start = ((bf16[64,4,1029]{2,1,0:T(4,128)(2,1)}), bf16[64,4,1029]{2,1,0:T(4,128)(2,1)S(1)}, u32[]{:S(2)}, u32[]{:S(2)}) async-start(bf16[64,4,1029]{2,1,0:T(4,128)(2,1)} %get-tuple-element.14), calls=%async_computation | async-start | bytes 1179648 | tf_op jit(solution)/shard_map/all_to_all | solution.py:282
  15.8 11.5 %collective-permute-start = (bf16[16,1029]{1,0:T(8,128)(2,1)}, bf16[16,1029]{1,0:T(8,128)(2,1)S(1)}, u32[]{:S(2)}, u32[]{:S(2)}) collective-permute-start(bf16[16,1029]{1,0:T(8,128)(2,1)} %get-tuple-element.11), channel_id=1, source_target_pairs={{0,64},{64,128},{128,192},{1,65},{65,129},{129,193},{2,66},{66,130... | collective-permute-start | bytes 98792 | tf_op jit(solution)/shard_map/ppermute | solution.py:286
  19.0 8.4 %collective-permute-start.1 = (bf16[16,1029]{1,0:T(8,128)(2,1)}, bf16[16,1029]{1,0:T(8,128)(2,1)S(1)}, u32[]{:S(2)}, u32[]{:S(2)}) collective-permute-start(bf16[16,1029]{1,0:T(8,128)(2,1)} %get-tuple-element.12), channel_id=1, source_target_pairs={{64,0},{128,64},{192,128},{65,1},{129,65},{193,129},{66,2},{130,66... | collective-permute-start | bytes 98792 | tf_op jit(solution)/shard_map/ppermute | solution.py:287

commit v5 on v4

--- a/solution.py
+++ b/solution.py
@@ -182,9 +182,9 @@
         return pltpu.make_async_copy(total.at[comp], out_hbm.at[comp], out_sems.at[comp])
 
     for comp in range(comps):
-        fetch(comp).start()
-    for comp in range(comps):
-        fetch_near(comp).start()
+        fetch(comp).start(priority=int(comp > 0))
+    for comp in range(comps):
+        fetch_near(comp).start(priority=1)
     source[...] = g_ref[...].reshape(source.shape[1], source.shape[0]).T
     place = lax.broadcasted_iota(jnp.int32, (wide, nboxes), 0) + (nboxes + 2 * FACE)
     for d in range(dirs):

time: 42.8 us -> 42.9 us (level)
  no operation moved by 1% of the time
where the time goes in v5:
time: 42.9 us; the launch traced here: 42.6 us
  Pallas kernels  23.9 us (56%)
  starting transfers between devices  17.6 us (41%)
  waiting for transfers between devices  1.09 us (3%)
    all_to_all x1, starting transfers between devices, local(): ghost = lax.all_to_all(table, 'owner', 0, 0, tiled=True)  13.1 us
    pallas_call x1, Pallas kernels, far_sum(): pl.pallas_call(far_kernel, out_shape=jax.ShapeDtypeStruct((comps, nodes,...  7.77 us
    pallas_call x1, Pallas kernels, near_sum(): pl.pallas_call(own_kernel, out_shape=(jax.ShapeDtypeStruct(shape, jnp.flo...  7.04 us
    pallas_call x1, Pallas kernels, near_sum(): pl.pallas_call(rim_kernel, out_shape=pltpu.MemorySpace.HBM(shape, jnp.flo...  6.41 us
    ppermute x1, starting transfers between devices, local(): low = lax.ppermute(low, 'leaf', forward)  3.12 us
    pallas_call x1, Pallas kernels, make_table(): pl.pallas_call(table_kernel, out_shape=(jax.ShapeDtypeStruct((owners, cap...  2.68 us
    ppermute x1, starting transfers between devices, local(): high = lax.ppermute(high, 'leaf', backward)  1.29 us
    all_to_all x1, waiting for transfers between devices, local(): ghost = lax.all_to_all(table, 'owner', 0, 0, tiled=True)  1.09 us
  transfers between devices with their start and end apart: 3, of which 1 were waited for; matrix products, arithmetic and copies ran while one was open for 0% of the time, Pallas kernels for 32%

profile of v5, /device:TPU:1, one launch (start us, length us, event | category | flops | bytes accessed | tf_op | source)
XLA Modules:
  0.0 42.6 jit_solution(6419468281540464999)
XLA Ops:
  0.0 0.0 copy-start
  0.0 0.0 copy-start.1
  0.0 2.7 %table.1 = (bf16[64,4,1029]{2,1,0:T(4,128)(2,1)}, bf16[16,1029]{1,0:T(8,128)(2,1)}, bf16[16,1029]{1,0:T(8,128)(2,1)}) custom-call(f32[3,343,384]{2,1,0:T(8,128)} %m_hbm.3, f32[3,343,384]{2,1,0:T(8,128)} %m_hbm.3, s32[4,64]{1,0:T(4,128)} %bitcast.10), custom_call_target="tpu_custom_call" | custom-call | tf_op jit(solution)/shard_map/table/pallas_call | solution.py:46
  2.7 13.1 %all-to-all-start = ((bf16[64,4,1029]{2,1,0:T(4,128)(2,1)}), bf16[64,4,1029]{2,1,0:T(4,128)(2,1)S(1)}, u32[]{:S(2)}, u32[]{:S(2)}) async-start(bf16[64,4,1029]{2,1,0:T(4,128)(2,1)} %get-tuple-element.14), calls=%async_computation | async-start | bytes 1179648 | tf_op jit(solution)/shard_map/all_to_all | solution.py:282
  15.8 3.1 %collective-permute-start = (bf16[16,1029]{1,0:T(8,128)(2,1)}, bf16[16,1029]{1,0:T(8,128)(2,1)S(1)}, u32[]{:S(2)}, u32[]{:S(2)}) collective-permute-start(bf16[16,1029]{1,0:T(8,128)(2,1)} %get-tuple-element.11), channel_id=1, source_target_pairs={{0,64},{64,128},{128,192},{1,65},{65,129},{129,193},{2,66},{66,130... | collective-permute-start | bytes 98792 | tf_op jit(solution)/shard_map/ppermute | solution.py:286
  19.0 1.3 %collective-permute-start.1 = (bf16[16,1029]{1,0:T(8,128)(2,1)}, bf16[16,1029]{1,0:T(8,128)(2,1)S(1)}, u32[]{:S(2)}, u32[]{:S(2)}) collective-permute-start(bf16[16,1029]{1,0:T(8,128)(2,1)} %get-tuple-element.12), channel_id=1, source_target_pairs={{64,0},{128,64},{192,128},{65,1},{129,65},{193,129},{66,2},{130,66... | collective-permute-start | bytes 98792 | tf_op jit(solution)/shard_map/ppermute | solution.py:287
  20.3 0.0 copy-done
  20.3 0.0 copy-done.1
  20.3 7.0 %own.1 = (f32[3,343,384]{2,1,0:T(8,128)S(1)}, bf16[1029,4,1029]{2,1,0:T(4,128)(2,1)S(1)}) custom-call(f32[3,343,384]{2,1,0:T(8,128)S(1)} %copy-done, s32[4,384]{1,0:T(4,128)S(1)} %bitcast.5, bf16[1029,4,1029]{2,1,0:T(4,128)(2,1)} %bitcast.8), custom_call_target="tpu_custom_call" | custom-call | tf_op jit(solution)/shard_map/own/pallas_call | solution.py:231
  27.3 0.0 collective-permute-done.low_ref
  27.3 0.0 collective-permute-done.1.high_ref
  27.4 6.4 %rim.1.near_hbm = f32[3,343,384]{2,1,0:T(8,128)} custom-call(f32[3,343,384]{2,1,0:T(8,128)S(1)} %get-tuple-element.10.part_hbm, f32[3,343,384]{2,1,0:T(8,128)S(1)} %copy-done, bf16[16,1029]{1,0:T(8,128)(2,1)S(1)} %collective-permute-done.low_ref, bf16[16,1029]{1,0:T(8,128)(2,1)S(1)} %collective-permute-done.1.high_ref, s32[4,384]{1,0:T(4,128)S(1)} %bitcast.6, ...), custom_call_target="tpu_custom_call" | custom-call | tf_op jit(solution)/shard_map/rim/pallas_call | solution.py:243
  33.8 1.1 %all-to-all-done.g_ref = bf16[64,4,1029]{2,1,0:T(4,128)(2,1)S(1)} async-done(((bf16[64,4,1029]{2,1,0:T(4,128)(2,1)}), bf16[64,4,1029]{2,1,0:T(4,128)(2,1)S(1)}, u32[]{:S(2)}, u32[]{:S(2)}) %all-to-all-start) | async-done | bytes 526880 | tf_op jit(solution)/shard_map/all_to_all | solution.py:282
  34.9 7.8 %far.1 = f32[3,343,384]{2,1,0:T(8,128)} custom-call(f32[3,343,384]{2,1,0:T(8,128)} %rim.1.near_hbm, bf16[64,4,1029]{2,1,0:T(4,128)(2,1)S(1)} %all-to-all-done.g_ref, s32[4,384]{1,0:T(4,128)S(1)} %bitcast.7, bf16[1029,4,1029]{2,1,0:T(4,128)(2,1)} %bitcast.9), custom_call_target="tpu_custom_call" | custom-call | tf_op jit(solution)/shard_map/far/pallas_call | solution.py:259
Async XLA Ops:
  0.0 20.3 %copy-start = (f32[3,343,384]{2,1,0:T(8,128)S(1)}, f32[3,343,384]{2,1,0:T(8,128)}, u32[]{:S(2)}) copy-start(f32[3,343,384]{2,1,0:T(8,128)} %m_hbm.3) | copy-start | bytes 4741636
  0.0 20.3 %copy-start.1 = (s32[384,4]{0,1:T(4,128)S(1)}, s32[384,4]{0,1:T(4,128)}, u32[]{:S(2)}) copy-start(s32[384,4]{0,1:T(4,128)} %param.6) | copy-start | bytes 18436
  2.7 32.2 %all-to-all-start = ((bf16[64,4,1029]{2,1,0:T(4,128)(2,1)}), bf16[64,4,1029]{2,1,0:T(4,128)(2,1)S(1)}, u32[]{:S(2)}, u32[]{:S(2)}) async-start(bf16[64,4,1029]{2,1,0:T(4,128)(2,1)} %get-tuple-element.14), calls=%async_computation | async-start | bytes 1179648 | tf_op jit(solution)/shard_map/all_to_all | solution.py:282
  15.8 11.5 %collective-permute-start = (bf16[16,1029]{1,0:T(8,128)(2,1)}, bf16[16,1029]{1,0:T(8,128)(2,1)S(1)}, u32[]{:S(2)}, u32[]{:S(2)}) collective-permute-start(bf16[16,1029]{1,0:T(8,128)(2,1)} %get-tuple-element.11), channel_id=1, source_target_pairs={{0,64},{64,128},{128,192},{1,65},{65,129},{129,193},{2,66},{66,130... | collective-permute-start | bytes 98792 | tf_op jit(solution)/shard_map/ppermute | solution.py:286
  19.0 8.4 %collective-permute-start.1 = (bf16[16,1029]{1,0:T(8,128)(2,1)}, bf16[16,1029]{1,0:T(8,128)(2,1)S(1)}, u32[]{:S(2)}, u32[]{:S(2)}) collective-permute-start(bf16[16,1029]{1,0:T(8,128)(2,1)} %get-tuple-element.12), channel_id=1, source_target_pairs={{64,0},{128,64},{192,128},{65,1},{129,65},{193,129},{66,2},{130,66... | collective-permute-start | bytes 98792 | tf_op jit(solution)/shard_map/ppermute | solution.py:287
